TPU v7x, 512 devices: a whole 4x8x8 slice. The times are simulated.
512 devices in a mesh: dp: 8 (over z), frame: 32 (over y_hi, x, core), tile: 2 (over y_lo).
Axes of the slice: x: 4, y: 8 (y_hi: 4, y_lo: 2; y = y_hi * 2 + y_lo), z: 8, core: 2. Of those that a mesh axis runs over, the one named last changes fastest.
Arguments:
- clip_input: bfloat16 [8, 32, 18, 32, 640], P('dp', 'frame', 'tile'), may hold values from -36 to 36
- cotangent: bfloat16 [8, 32, 18, 32, 640], P('dp', 'frame', 'tile'), may hold values from -6 to 6
- norm_gain: float32 [640], replicated, may hold values from 0.25 to 1.75
- conv_weight: bfloat16 [9, 640, 640], P(None, ('frame', 'tile')), may hold values from -0.078125 to 0.078125
- attn_weight: bfloat16 [640, 2560], P(('frame', 'tile')), may hold values from -0.25 to 0.25
- query_gain: float32 [64], replicated, may hold values from 0.5 to 1.5
- key_gain: float32 [64], replicated, may hold values from 0.5 to 1.5
- logit_scale: float32 [10], replicated, may hold values from 0.5 to 4
Outputs:
- mid_grad: bfloat16 [8, 32, 18, 32, 640], P('dp', 'frame', 'tile')
- value_grad: float32 [640, 640], P(('frame', 'tile'))
- out_proj_grad: float32 [640, 640], P(('frame', 'tile'))
- query_gain_grad: float32 [64], replicated
- key_gain_grad: float32 [64], replicated
- scale_grad: float32 [10], replicated
All inputs are finite; a program needn't handle non-finite values.
Results may differ from a plain program's by a relative error of at most 0.013.
The roundings to bfloat16 on the way count: a program that leaves them out, or rounds other values in their place, can miss the bound.
Values may be sent and summed in bfloat16 or wider, within the bound.
A program may use at most 128 MiB of HBM per device.

v0:
```python
import math
import jax
import jax.numpy as jnp
from jax import lax
from jax.sharding import PartitionSpec as P

GROUPS = 32


def extended(x, sides, width):
    for axis, dim in sides:
        devices, length = (lax.axis_size(axis), x.shape[dim])
        up = [(i, (i + 1) % devices) for i in range(devices - 1)]
        down = [(j, i) for i, j in up]
        last = lax.slice_in_dim(x, length - width, length, axis=dim)
        first = lax.slice_in_dim(x, 0, width, axis=dim)
        before = lax.ppermute(last, axis, up)
        after = lax.ppermute(first, axis, down)
        x = jnp.concatenate([before, x, after], axis=dim)
    return x


def layer_stats(vec):
    mean = jnp.mean(vec, axis=-1, keepdims=True)
    cent = vec - mean
    var = jnp.mean(cent * cent, axis=-1, keepdims=True)
    rstd = lax.rsqrt(var + 1e-05)
    return (cent * rstd, rstd)


def layer_back(dhat, hat, rstd):
    first = jnp.mean(dhat, axis=-1, keepdims=True)
    second = jnp.mean(dhat * hat, axis=-1, keepdims=True)
    return rstd * (dhat - first - hat * second)


def attention_pass(mid, cot, weights, query_gain, key_gain, logit_scale):
    frames, count, width = mid.shape
    heads = logit_scale.shape[0]
    depth = width // heads
    total = frames * count
    high = lax.Precision.HIGHEST
    f32 = jnp.float32
    flat = mid.reshape(total, width)
    w_inner = weights[:, : 3 * width]
    proj = jnp.dot(flat, w_inner, preferred_element_type=f32)
    query = proj[:, :width].reshape(frames, count, heads, depth)
    keyed = proj[:, width : 2 * width].reshape(frames, count, heads, depth)
    value = proj[:, 2 * width :].astype(jnp.bfloat16).reshape(frames, count, heads, depth)
    q_hat, q_rstd = layer_stats(query)
    k_hat, k_rstd = layer_stats(keyed)
    q_norm = q_hat * query_gain
    k_norm = k_hat * key_gain
    root = math.sqrt(depth)
    raw = jnp.einsum("fnhd,gnhd->nhfg", q_norm, k_norm, precision=high) / root
    scale = logit_scale[None, :, None, None]
    expo = jnp.exp(raw * scale)
    probs = expo / jnp.sum(expo, axis=-1, keepdims=True)
    probs_b = probs.astype(jnp.bfloat16)
    mixed = jnp.einsum("nhfg,gnhd->fnhd", probs_b, value, preferred_element_type=f32)
    mixed = mixed.astype(jnp.bfloat16).reshape(total, width)
    cot_flat = cot.reshape(total, width)
    w_out = weights[:, 3 * width :]
    d_mixed = lax.dot_general(cot_flat, w_out, (((1,), (1,)), ((), ())), preferred_element_type=f32)
    d_mixed = d_mixed.astype(jnp.bfloat16).reshape(frames, count, heads, depth)
    d_probs = jnp.einsum("fnhd,gnhd->nhfg", d_mixed, value, preferred_element_type=f32)
    d_value = jnp.einsum("nhfg,fnhd->gnhd", probs_b, d_mixed, preferred_element_type=f32)
    d_value = d_value.astype(jnp.bfloat16)
    d_logits = probs * (d_probs - jnp.sum(probs * d_probs, axis=-1, keepdims=True))
    scale_term = jnp.sum(d_logits * raw, axis=(0, 2, 3))
    d_raw = d_logits * scale / root
    d_qn = jnp.einsum("nhfg,gnhd->fnhd", d_raw, k_norm, precision=high)
    d_kn = jnp.einsum("nhfg,fnhd->gnhd", d_raw, q_norm, precision=high)
    qgain_term = jnp.sum(d_qn * q_hat, axis=(0, 1, 2))
    kgain_term = jnp.sum(d_kn * k_hat, axis=(0, 1, 2))
    d_query = layer_back(d_qn * query_gain, q_hat, q_rstd).astype(jnp.bfloat16)
    d_key = layer_back(d_kn * key_gain, k_hat, k_rstd).astype(jnp.bfloat16)
    d_cat = jnp.concatenate(
        [d_query.reshape(total, width), d_key.reshape(total, width), d_value.reshape(total, width)],
        axis=1,
    )
    d_mid = lax.dot_general(d_cat, w_inner, (((1,), (1,)), ((), ())), preferred_element_type=f32)
    d_mid = d_mid.astype(jnp.bfloat16).reshape(frames, count, width)
    return (d_mid, mixed, d_value.reshape(total, width), scale_term, qgain_term, kgain_term)


def local(
    clip_input, cotangent, norm_gain, conv_weight, attn_weight, query_gain, key_gain, logit_scale
):
    source = clip_input[0]
    cot = cotangent[0]
    frames_here, rows, cols, width = source.shape
    positions = rows * cols
    per_group = width // GROUPS
    cot_flat = cot.reshape(frames_here, positions, width)
    attn_full = lax.all_gather(attn_weight, ("frame", "tile"), axis=0, tiled=True)
    xf = source.astype(jnp.float32).reshape(frames_here, positions, GROUPS, per_group)
    sums, squares = lax.psum((jnp.sum(xf, axis=(1, 3)), jnp.sum(xf * xf, axis=(1, 3))), "tile")
    count = positions * lax.axis_size("tile") * per_group
    mean = sums / count
    rstd = lax.rsqrt(squares / count - mean * mean + 1e-05)
    normed = (xf - mean[:, None, :, None]) * rstd[:, None, :, None]
    zed = normed.reshape(frames_here, rows, cols, width) * norm_gain
    act = jax.nn.silu(zed).astype(jnp.bfloat16)
    padded = extended(act, (("tile", 1),), 1)
    padded = jnp.pad(padded, ((0, 0), (0, 0), (1, 1), (0, 0)))
    slabs = []
    for row_off in (-1, 0, 1):
        for col_off in (-1, 0, 1):
            slabs.append(
                padded[:, 1 + row_off : 1 + row_off + rows, 1 + col_off : 1 + col_off + cols, :]
            )
    stacked = jnp.stack(slabs, axis=3).reshape(frames_here * positions, 9, width)
    full_conv = lax.all_gather(conv_weight, ("frame", "tile"), axis=1, tiled=True)
    pre = jnp.dot(
        stacked.reshape(frames_here * positions, 9 * width),
        full_conv.reshape(9 * width, width),
        preferred_element_type=jnp.float32,
    )
    mid = (source.astype(jnp.float32) + pre.reshape(frames_here, rows, cols, width)).astype(
        jnp.bfloat16
    )
    mid_flat = mid.reshape(frames_here, positions, width)
    mid_tiled, cot_tiled = (
        lax.all_to_all(mid_flat, "frame", split_axis=1, concat_axis=0, tiled=True),
        lax.all_to_all(cot_flat, "frame", split_axis=1, concat_axis=0, tiled=True),
    )
    d_mid, mixed, d_value, scale_term, qgain_term, kgain_term = attention_pass(
        mid_tiled, cot_tiled, attn_full, query_gain, key_gain, logit_scale
    )
    d_back = lax.all_to_all(d_mid, "frame", split_axis=0, concat_axis=1, tiled=True)
    mid_grad = (
        cot.astype(jnp.float32) + d_back.reshape(frames_here, rows, cols, width).astype(jnp.float32)
    ).astype(jnp.bfloat16)
    tiled_mid = mid_tiled.reshape(-1, width)
    tiled_cot = cot_tiled.reshape(-1, width)
    contract = (((0,), (0,)), ((), ()))
    value_term = lax.dot_general(tiled_mid, d_value, contract, preferred_element_type=jnp.float32)
    out_term = lax.dot_general(mixed, tiled_cot, contract, preferred_element_type=jnp.float32)
    shares = lax.psum_scatter(
        jnp.concatenate([value_term, out_term], axis=1),
        ("frame", "tile"),
        scatter_dimension=0,
        tiled=True,
    )
    summed = lax.psum(shares.astype(jnp.bfloat16), "dp").astype(jnp.float32)
    scale_sum, qgain_sum, kgain_sum = lax.psum(
        (scale_term, qgain_term, kgain_term), ("dp", "frame", "tile")
    )
    tokens_all = lax.axis_size("dp") * mid_tiled.shape[0] * rows * lax.axis_size("tile") * cols
    factor = 1.0 / math.sqrt(tokens_all)
    value_grad = summed[:, :width] * factor
    out_proj_grad = summed[:, width:] * factor
    return (
        mid_grad[None],
        value_grad,
        out_proj_grad,
        qgain_sum * factor,
        kgain_sum * factor,
        scale_sum * factor,
    )


def solution(mesh):
    in_specs = (
        P("dp", "frame", "tile", None, None),
        P("dp", "frame", "tile", None, None),
        P(),
        P(None, ("frame", "tile"), None),
        P(("frame", "tile"), None),
        P(),
        P(),
        P(),
    )
    out_specs = (
        P("dp", "frame", "tile", None, None),
        P(("frame", "tile"), None),
        P(("frame", "tile"), None),
        P(),
        P(),
        P(),
    )
    return jax.shard_map(local, mesh=mesh, in_specs=in_specs, out_specs=out_specs, check_vma=False)
```

profile of v0, /device:TPU:1, one launch (start us, length us, event | category | flops | bytes accessed | tf_op | source)
XLA Modules:
  0.0 950.0 jit_solution(8612890330028750961)
XLA Ops:
  11.2 4.4 all-reduce.3
  17.0 3.4 collective-permute-start
  26.9 11.3 %all-to-all-start.1 = ((bf16[32,2,2880]{2,1,0:T(2,128)(2,1)}), bf16[32,2,2880]{2,1,0:T(2,128)(2,1)S(1)}, u32[]{:S(2)}, u32[]{:S(2)}) async-start(bf16[32,2,2880]{2,1,0:T(2,128)(2,1)} %reshape.273), calls=%async_computation.1 | async-start | bytes 753664 | tf_op jit(solution)/shard_map/all_to_all | solution.py:126
  39.7 4.1 copy.126
  43.9 7.3 dot_general.38
  51.2 167.2 %all-gather.4.cloned.1.call-done = bf16[9,640,640]{2,0,1:T(8,128)(2,1)} async-done(((bf16[9,10,640]{2,0,1:T(8,128)(2,1)}), bf16[9,640,640]{2,0,1:T(8,128)(2,1)}) %all-gather.4.cloned.1.call-update) | async-done | bytes 7372816 | tf_op jit(solution)/shard_map/all_gather | solution.py:114
  218.4 9.3 copy.128
  227.7 6.9 fusion.26
  235.2 2.9 reduce.9
  239.2 16.7 %all-to-all-start = ((bf16[32,2,2880]{2,1,0:T(2,128)(2,1)}), bf16[32,2,2880]{2,1,0:T(2,128)(2,1)}, u32[]{:S(2)}, u32[]{:S(2)}) async-start(bf16[32,2,2880]{2,1,0:T(2,128)(2,1)} %reshape.275), calls=%async_computation | async-start | bytes 753664 | tf_op jit(solution)/shard_map/all_to_all | solution.py:125
  259.2 164.3 %all-gather.6.cloned.1.call-done = bf16[64,10,2560]{2,1,0:T(8,128)(2,1)} async-done(((bf16[1,10,2560]{2,1,0:T(8,128)(2,1)}), bf16[64,10,2560]{2,1,0:T(8,128)(2,1)}) %all-gather.6.cloned.1.call-update) | async-done | bytes 3276816 | tf_op jit(solution)/shard_map/all_gather | solution.py:96
  423.4 5.3 reshape.268
  428.7 2.9 convolution_convert_fusion.2
  434.2 3.6 reshape.276
  447.5 5.0 multiply_reduce_fusion.4
  453.3 3.0 fusion.18
  458.4 3.0 multiply_reduce_fusion
  461.4 4.5 fusion.5
  465.9 5.9 fusion.6
  485.0 284.3 %all-reduce.5 = bf16[640,1280]{0,1:T(8,128)(2,1)} all-reduce(f32[640,1280]{0,1:T(8,128)} %pad_maximum_fusion), channel_id=2, replica_groups=mesh['dp'=8,'frame'=32,'tile'=2] {'frame','tile'}, use_global_device_ids=true, to_apply=%region_16.17.clone | all-reduce | flops 819200 | bytes 4915200
  770.5 28.1 %psum.44 = bf16[10,1280]{0,1:T(8,128)(2,1)} all-reduce(bf16[10,1280]{0,1:T(8,128)(2,1)S(1)} %dynamic-slice_convert_fusion), channel_id=1, replica_groups=mesh['dp'=8,'frame'=32,'tile'=2] {'dp'}, use_global_device_ids=true, to_apply=%region_17.18 | all-reduce | flops 12800 | bytes 51200 | tf_op jit(solution)/shard_map/psum | solution.py:146
  814.1 3.1 fusion.23
  819.2 18.8 %all-to-all-start.2 = ((bf16[32,9,640]{2,1,0:T(8,128)(2,1)}), bf16[32,9,640]{2,1,0:T(8,128)(2,1)S(1)}, u32[]{:S(2)}, u32[]{:S(2)}) async-start(bf16[32,9,640]{2,1,0:T(8,128)(2,1)} %reshape.261), calls=%async_computation.2 | async-start | bytes 1310720 | tf_op jit(solution)/shard_map/all_to_all | solution.py:131
  839.6 100.9 %all-reduce.2 = (f32[64]{0:T(128)S(1)}, f32[64]{0:T(128)S(1)}, f32[10]{0:T(128)S(1)}) all-reduce(f32[64]{0:T(128)S(1)} %get-tuple-element.44, f32[64]{0:T(128)S(1)} %get-tuple-element.42, f32[10]{0:T(128)S(1)} %copy-done.18), channel_id=1, replica_groups=mesh['dp'=8,'frame'=32,'tile'=2] {'dp','frame','tile'}, use_global_device_ids=true, to_apply=%region_19.20 | all-reduce | flops 138 | bytes 1104 | tf_op jit(solution)/shard_map/psum | solution.py:147
  (126 shorter events, 68.3 us)
Async XLA Ops:
  7.2 8.9 copy-start.7
  7.2 14.5 %copy-start.12 = (bf16[1,1,9,32,640]{4,3,2,1,0:T(8,128)(2,1)S(1)}, bf16[1,1,9,32,640]{4,3,2,1,0:T(8,128)(2,1)}, u32[]{:S(2)}) copy-start(bf16[1,1,9,32,640]{4,3,2,1,0:T(8,128)(2,1)} %param.9) | copy-start | bytes 1105924
  7.2 211.2 %all-gather.4.cloned.1.call-start = ((), (), s32[]{:S(2)}) async-start(), calls=%async_computation.3 | async-start | bytes 13312000 | tf_op jit(solution)/shard_map/all_gather | solution.py:114
  9.0 414.5 %all-gather.6.cloned.1.call-start = ((), (), s32[]{:S(2)}) async-start(), calls=%async_computation.4 | async-start | bytes 5324800 | tf_op jit(solution)/shard_map/all_gather | solution.py:96
  17.0 21.2 %collective-permute-start = (bf16[1,1,32,640]{3,2,1,0:T(8,128)(2,1)S(1)}, bf16[1,1,32,640]{3,2,1,0:T(8,128)(2,1)S(1)}, u32[]{:S(2)}, u32[]{:S(2)}) collective-permute-start(bf16[1,1,32,640]{3,2,1,0:T(8,128)(2,1)S(1)} %get-tuple-element.63), channel_id=1, source_target_pairs={{0,1},{2,3},{4,5},{6,7},{8,9},{10,11},{12,13},{14,15},{16,17},{18,... | collective-permute-start | bytes 122888 | tf_op jit(solution)/shard_map/ppermute | solution.py:17
  20.4 17.8 %collective-permute-start.1 = (bf16[1,1,32,640]{3,2,1,0:T(8,128)(2,1)S(1)}, bf16[1,1,32,640]{3,2,1,0:T(8,128)(2,1)S(1)}, u32[]{:S(2)}, u32[]{:S(2)}) collective-permute-start(bf16[1,1,32,640]{3,2,1,0:T(8,128)(2,1)S(1)} %get-tuple-element.64), channel_id=1, source_target_pairs={{1,0},{3,2},{5,4},{7,6},{9,8},{11,10},{13,12},{15,14},{17,16},{19,... | collective-permute-start | bytes 122888 | tf_op jit(solution)/shard_map/ppermute | solution.py:18
  26.9 212.4 %all-to-all-start.1 = ((bf16[32,2,2880]{2,1,0:T(2,128)(2,1)}), bf16[32,2,2880]{2,1,0:T(2,128)(2,1)S(1)}, u32[]{:S(2)}, u32[]{:S(2)}) async-start(bf16[32,2,2880]{2,1,0:T(2,128)(2,1)} %reshape.273), calls=%async_computation.1 | async-start | bytes 753664 | tf_op jit(solution)/shard_map/all_to_all | solution.py:126
  38.4 0.7 copy-start.14
  235.1 22.7 %copy-start.17 = (f32[10]{0:T(128)S(1)}, f32[10]{0:T(128)}, u32[]{:S(2)}) copy-start(f32[10]{0:T(128)} %param.15) | copy-start | bytes 124
  239.2 194.9 %all-to-all-start = ((bf16[32,2,2880]{2,1,0:T(2,128)(2,1)}), bf16[32,2,2880]{2,1,0:T(2,128)(2,1)}, u32[]{:S(2)}, u32[]{:S(2)}) async-start(bf16[32,2,2880]{2,1,0:T(2,128)(2,1)} %reshape.275), calls=%async_computation | async-start | bytes 753664 | tf_op jit(solution)/shard_map/all_to_all | solution.py:125
  428.7 9.0 copy-start.2
  444.1 1.5 copy-start
  446.1 1.4 copy-start.1
  447.5 5.1 copy-start.8
  447.5 5.1 copy-start.9
  480.3 2.8 copy-start.11
  480.3 2.1 copy-start.6
  798.7 4.7 copy-start.5
  804.8 3.9 copy-start.4
  810.1 4.0 copy-start.3
  817.1 20.8 %copy-start.10 = (f32[10,1280]{0,1:T(8,128)S(1)}, f32[10,1280]{0,1:T(8,128)}, u32[]{:S(2)}) copy-start(f32[10,1280]{0,1:T(8,128)} %convert_element_type.150) | copy-start | bytes 153604
  819.2 20.4 %copy-start.18 = (f32[10]{0:T(128)S(1)}, f32[10]{0:T(128)}, u32[]{:S(2)}) copy-start(f32[10]{0:T(128)} %get-tuple-element.71) | copy-start | bytes 124
  819.2 122.8 %all-to-all-start.2 = ((bf16[32,9,640]{2,1,0:T(8,128)(2,1)}), bf16[32,9,640]{2,1,0:T(8,128)(2,1)S(1)}, u32[]{:S(2)}, u32[]{:S(2)}) async-start(bf16[32,9,640]{2,1,0:T(8,128)(2,1)} %reshape.261), calls=%async_computation.2 | async-start | bytes 1310720 | tf_op jit(solution)/shard_map/all_to_all | solution.py:131
  837.9 104.2 %copy-start.13 = (bf16[1,1,9,32,640]{4,3,2,1,0:T(8,128)(2,1)S(1)}, bf16[1,1,9,32,640]{4,3,2,1,0:T(8,128)(2,1)}, u32[]{:S(2)}) copy-start(bf16[1,1,9,32,640]{4,3,2,1,0:T(8,128)(2,1)} %param.9) | copy-start | bytes 1105924
  (2 other events, 1.3 us)
Sparse Core Ops, SparseCore 0:
  10.7 207.6 all-gather.3
  220.5 202.8 all-gather.5
where the time goes:
time: 956 us; the launch traced here: 950 us
  blocking collectives  418 us (44%)
  waiting for transfers between devices  332 us (35%)
  local copies, waits for them, and re-layouts  69.5 us (7%)
  starting transfers between devices  51.6 us (5%)
  matrix products  33.7 us (4%)
  other arithmetic  29.8 us (3%)
  between operations  15.5 us (2%)
    unnamed x1, blocking collectives  284 us
    all_gather x1, waiting for transfers between devices, local(): lax.all_gather(conv_weight, ('frame', 'tile'), axis=1, tiled=True)  167 us
    all_gather x1, waiting for transfers between devices, local(): lax.all_gather(attn_weight, ('frame', 'tile'), axis=0, tiled=True)  164 us
    psum x1, blocking collectives, local(): lax.psum((scale_term, qgain_term, kgain_term), ('dp', 'frame', 'tile'))  101 us
    psum x1, blocking collectives, local(): summed = lax.psum(shares.astype(jnp.bfloat16), 'dp').astype(jnp.float32)  28.1 us
    unnamed x53, local copies, waits for them, and re-layouts  19.7 us
  transfers between devices with their start and end apart: 7, of which 2 were waited for; matrix products, arithmetic and copies ran while one was open for 6% of the time, Pallas kernels for 0%

commit v1 on v0

--- a/solution.py
+++ b/solution.py
@@ -93,7 +93,10 @@
     positions = rows * cols
     per_group = width // GROUPS
     cot_flat = cot.reshape(frames_here, positions, width)
-    attn_full = lax.all_gather(attn_weight, ("frame", "tile"), axis=0, tiled=True)
+    size = lax.axis_size(("frame", "tile"))
+    blocks = jnp.stack([attn_weight for _ in range(size)])
+    blocks = lax.all_to_all(blocks, ("frame", "tile"), split_axis=0, concat_axis=0)
+    attn_full = jnp.concatenate(blocks, axis=0)
     xf = source.astype(jnp.float32).reshape(frames_here, positions, GROUPS, per_group)
     sums, squares = lax.psum((jnp.sum(xf, axis=(1, 3)), jnp.sum(xf * xf, axis=(1, 3))), "tile")
     count = positions * lax.axis_size("tile") * per_group

time: 956 us -> 869 us (0.909)
  waiting for transfers between devices: 332 us -> 90.2 us
  blocking collectives: 418 us -> 582 us
  starting transfers between devices: 51.6 us -> 40.4 us
    all_gather x1 -> x0, waiting for transfers between devices: 164 us -> none  [local(): lax.all_gather(attn_weight, ('frame', 'tile'), axis=0, tiled=True)]
    psum x1, blocking collectives: 4.43 us -> 137 us  [local(): lax.psum((jnp.sum(xf, axis=(1, 3)), jnp.sum(xf * xf, axis=(1, 3))), 'tile')]
    all_gather x1, waiting for transfers between devices: 167 us -> 85.4 us  [local(): lax.all_gather(conv_weight, ('frame', 'tile'), axis=1, tiled=True)]
    all_to_all x0 -> x1, blocking collectives: none -> 26.4 us  [local(): lax.all_to_all(cot_flat, 'frame', split_axis=1, concat_axis=0, tiled=True)]
    unnamed x53 -> x52, local copies, waits for them, and re-layouts: 19.7 us -> 13.2 us
  transfers between devices with their start and end apart: 7 -> 6, of which waited for: 2 -> 3; matrix products, arithmetic and copies ran while one was open for 6% -> 7% of each run, Pallas kernels for 0% -> 0%
where the time goes in v1:
time: 869 us; the launch traced here: 863 us
  blocking collectives  582 us (67%)
  waiting for transfers between devices  90.2 us (10%)
  local copies, waits for them, and re-layouts  72.3 us (8%)
  starting transfers between devices  40.4 us (5%)
  matrix products  33.7 us (4%)
  other arithmetic  28.4 us (3%)
  between operations  15.4 us (2%)
    unnamed x1, blocking collectives  283 us
    psum x1, blocking collectives, local(): lax.psum((jnp.sum(xf, axis=(1, 3)), jnp.sum(xf * xf, axis=(1, 3))), 'tile')  137 us
    psum x1, blocking collectives, local(): lax.psum((scale_term, qgain_term, kgain_term), ('dp', 'frame', 'tile'))  103 us
    all_gather x1, waiting for transfers between devices, local(): lax.all_gather(conv_weight, ('frame', 'tile'), axis=1, tiled=True)  85.4 us
    psum x1, blocking collectives, local(): summed = lax.psum(shares.astype(jnp.bfloat16), 'dp').astype(jnp.float32)  33.1 us
    all_to_all x1, blocking collectives, local(): lax.all_to_all(cot_flat, 'frame', split_axis=1, concat_axis=0, tiled=True)  26.4 us
    all_to_all x1, starting transfers between devices, local(): lax.all_to_all(mid_flat, 'frame', split_axis=1, concat_axis=0, tiled=True)  18.5 us
  transfers between devices with their start and end apart: 6, of which 3 were waited for; matrix products, arithmetic and copies ran while one was open for 7% of the time, Pallas kernels for 0%

profile of v1, /device:TPU:1, one launch (start us, length us, event | category | flops | bytes accessed | tf_op | source)
XLA Modules:
  0.0 862.7 jit_solution(3128331483565893203)
XLA Ops:
  14.3 26.4 %all_to_all.32 = bf16[32,2,2880]{2,1,0:T(2,128)(2,1)S(1)} all-to-all(bf16[32,2,2880]{2,1,0:T(2,128)(2,1)S(1)} %reshape.277), channel_id=1, replica_groups=mesh['dp'=8,'frame'=32,'tile'=2] {'frame'}, dimensions={0} | all-to-all | bytes 737280 | tf_op jit(solution)/shard_map/all_to_all | solution.py:129
  40.7 3.0 stack.29
  43.7 5.7 all-to-all-start.1
  50.0 136.5 %all-reduce.3 = (f32[1,32]{1,0:T(1,128)S(1)}, f32[1,32]{1,0:T(1,128)S(1)}) all-reduce(f32[1,32]{1,0:T(1,128)S(1)} %bitcast.154, f32[1,32]{1,0:T(1,128)S(1)} %bitcast.153), channel_id=1, replica_groups=mesh['dp'=8,'frame'=32,'tile'=2] {'tile'}, use_global_device_ids=true, to_apply=%region_5.6 | all-reduce | flops 64 | bytes 512 | tf_op jit(solution)/shard_map/psum | solution.py:101
  189.9 4.1 collective-permute-done.1
  195.1 4.1 copy.126
  199.2 7.3 dot_general.38
  206.6 85.4 %all-gather.2.cloned.1.call-done = bf16[9,640,640]{2,0,1:T(8,128)(2,1)} async-done(((bf16[9,10,640]{2,0,1:T(8,128)(2,1)}), bf16[9,640,640]{2,0,1:T(8,128)(2,1)}) %all-gather.2.cloned.1.call-update) | async-done | bytes 7372816 | tf_op jit(solution)/shard_map/all_gather | solution.py:117
  292.0 9.3 %copy.128 = bf16[9,640,640]{2,1,0:T(8,128)(2,1)} copy(bf16[9,640,640]{2,0,1:T(8,128)(2,1)} %all-gather.2.cloned.1.call-done) | data formatting | bytes 14745600 | tf_op jit(solution)/shard_map/all_gather | solution.py:117
  301.3 6.9 fusion.26
  312.8 18.5 %all-to-all-start = ((bf16[32,2,2880]{2,1,0:T(2,128)(2,1)}), bf16[32,2,2880]{2,1,0:T(2,128)(2,1)}, u32[]{:S(2)}, u32[]{:S(2)}) async-start(bf16[32,2,2880]{2,1,0:T(2,128)(2,1)} %reshape.279), calls=%async_computation | async-start | bytes 753664 | tf_op jit(solution)/shard_map/all_to_all | solution.py:128
  334.6 5.3 reshape.258
  339.9 2.9 convolution_convert_fusion.2
  346.0 3.6 reshape.280
  359.4 5.3 multiply_reduce_fusion.4
  365.4 3.0 fusion.18
  370.5 3.0 multiply_reduce_fusion
  373.5 4.5 fusion.5
  378.0 5.9 fusion.6
  397.1 283.2 %all-reduce.5 = bf16[640,1280]{0,1:T(8,128)(2,1)} all-reduce(f32[640,1280]{0,1:T(8,128)} %pad_maximum_fusion), channel_id=2, replica_groups=mesh['dp'=8,'frame'=32,'tile'=2] {'frame','tile'}, use_global_device_ids=true, to_apply=%region_16.17.clone | all-reduce | flops 819200 | bytes 4915200
  681.5 33.1 %psum.44 = bf16[10,1280]{0,1:T(8,128)(2,1)} all-reduce(bf16[10,1280]{0,1:T(8,128)(2,1)S(1)} %dynamic-slice_convert_fusion), channel_id=1, replica_groups=mesh['dp'=8,'frame'=32,'tile'=2] {'dp'}, use_global_device_ids=true, to_apply=%region_17.18 | all-reduce | flops 12800 | bytes 51200 | tf_op jit(solution)/shard_map/psum | solution.py:149
  730.0 3.1 fusion.23
  735.1 13.3 %all-to-all-start.3 = ((bf16[32,9,640]{2,1,0:T(8,128)(2,1)}), bf16[32,9,640]{2,1,0:T(8,128)(2,1)S(1)}, u32[]{:S(2)}, u32[]{:S(2)}) async-start(bf16[32,9,640]{2,1,0:T(8,128)(2,1)} %reshape.267), calls=%async_computation.3 | async-start | bytes 1310720 | tf_op jit(solution)/shard_map/all_to_all | solution.py:134
  750.0 103.2 %all-reduce.2 = (f32[64]{0:T(128)S(1)}, f32[64]{0:T(128)S(1)}, f32[10]{0:T(128)S(1)}) all-reduce(f32[64]{0:T(128)S(1)} %get-tuple-element.44, f32[64]{0:T(128)S(1)} %get-tuple-element.42, f32[10]{0:T(128)S(1)} %copy-done.18), channel_id=1, replica_groups=mesh['dp'=8,'frame'=32,'tile'=2] {'dp','frame','tile'}, use_global_device_ids=true, to_apply=%region_19.20 | all-reduce | flops 138 | bytes 1104 | tf_op jit(solution)/shard_map/psum | solution.py:150
  (125 shorter events, 70.6 us)
Async XLA Ops:
  7.2 284.8 %all-gather.2.cloned.1.call-start = ((), (), s32[]{:S(2)}) async-start(), calls=%async_computation.4 | async-start | bytes 13312000 | tf_op jit(solution)/shard_map/all_gather | solution.py:117
  10.4 30.2 %copy-start.13 = (bf16[10,2560]{1,0:T(8,128)(2,1)S(1)}, bf16[10,2560]{1,0:T(8,128)(2,1)}, u32[]{:S(2)}) copy-start(bf16[10,2560]{1,0:T(8,128)(2,1)} %param.12) | copy-start | bytes 153604
  43.7 5.7 copy-start.7
  43.7 143.2 %copy-start.14 = (f32[640]{0:T(1024)S(1)}, f32[640]{0:T(1024)}, u32[]{:S(2)}) copy-start(f32[640]{0:T(1024)} %param.10) | copy-start | bytes 7684
  43.7 269.1 %all-to-all-start.1 = ((bf16[64,10,2560]{2,1,0:T(8,128)(2,1)}), bf16[64,10,2560]{2,1,0:T(8,128)(2,1)}, u32[]{:S(2)}, u32[]{:S(2)}) async-start(bf16[64,10,2560]{2,1,0:T(8,128)(2,1)} %stack.29), calls=%async_computation.1 | async-start | bytes 10485760 | tf_op jit(solution)/shard_map/all_to_all | solution.py:98
  187.2 2.8 collective-permute-start
  188.5 5.6 collective-permute-start.1
  308.7 24.6 %copy-start.17 = (f32[10]{0:T(128)S(1)}, f32[10]{0:T(128)}, u32[]{:S(2)}) copy-start(f32[10]{0:T(128)} %param.15) | copy-start | bytes 124
  312.8 33.2 %all-to-all-start = ((bf16[32,2,2880]{2,1,0:T(2,128)(2,1)}), bf16[32,2,2880]{2,1,0:T(2,128)(2,1)}, u32[]{:S(2)}, u32[]{:S(2)}) async-start(bf16[32,2,2880]{2,1,0:T(2,128)(2,1)} %reshape.279), calls=%async_computation | async-start | bytes 753664 | tf_op jit(solution)/shard_map/all_to_all | solution.py:128
  339.9 9.7 %copy-start.2 = (bf16[640,2560]{1,0:T(8,128)(2,1)}, bf16[640,2560]{1,0:T(8,128)(2,1)S(1)}, u32[]{:S(2)}) copy-start(bf16[640,2560]{1,0:T(8,128)(2,1)S(1)} %reshape.258) | copy-start | bytes 9830404
  356.0 1.5 copy-start
  358.0 1.4 copy-start.1
  359.4 5.4 copy-start.8
  359.4 5.4 copy-start.9
  364.7 0.7 copy-start.16
  392.4 2.8 copy-start.11
  392.4 2.1 copy-start.6
  714.6 4.7 copy-start.5
  720.7 3.9 copy-start.4
  726.0 4.0 copy-start.3
  733.1 15.3 %copy-start.10 = (f32[10,1280]{0,1:T(8,128)S(1)}, f32[10,1280]{0,1:T(8,128)}, u32[]{:S(2)}) copy-start(f32[10,1280]{0,1:T(8,128)} %convert_element_type.150) | copy-start | bytes 153604
  735.1 14.9 %copy-start.18 = (f32[10]{0:T(128)S(1)}, f32[10]{0:T(128)}, u32[]{:S(2)}) copy-start(f32[10]{0:T(128)} %get-tuple-element.71) | copy-start | bytes 124
  735.1 119.6 %all-to-all-start.3 = ((bf16[32,9,640]{2,1,0:T(8,128)(2,1)}), bf16[32,9,640]{2,1,0:T(8,128)(2,1)S(1)}, u32[]{:S(2)}, u32[]{:S(2)}) async-start(bf16[32,9,640]{2,1,0:T(8,128)(2,1)} %reshape.267), calls=%async_computation.3 | async-start | bytes 1310720 | tf_op jit(solution)/shard_map/all_to_all | solution.py:134
  748.4 106.5 %copy-start.12 = (bf16[1,1,9,32,640]{4,3,2,1,0:T(8,128)(2,1)S(1)}, bf16[1,1,9,32,640]{4,3,2,1,0:T(8,128)(2,1)}, u32[]{:S(2)}) copy-start(bf16[1,1,9,32,640]{4,3,2,1,0:T(8,128)(2,1)} %param.9) | copy-start | bytes 1105924
  (1 other events, 0.7 us)
Sparse Core Ops, SparseCore 0:
  10.7 281.2 all-gather.1
